TPU v7x, 32 devices: a whole 2x2x4 slice. The times are simulated.
32 devices in a mesh: row: 4 (over x, core), col: 8 (over z, y).
Axes of the slice: x: 2, y: 2, z: 4, core: 2. Of those that a mesh axis runs over, the one named last changes fastest.
Arguments:
- currents: float32 [3, 131072], P(None, ('row', 'col')), may hold values from -6 to 6
- probes: float32 [3, 131072], P(None, ('row', 'col')), may hold values from -6 to 6
- proj_weights: float32 [4, 131072], P(None, ('row', 'col')), may hold values from 0.5 to 2
- interp_weights: float32 [4, 131072], P(None, ('row', 'col')), may hold values from 0.5 to 2
- owner: int32 [131072, 1], P(('row', 'col')), may hold values from 0 to 31; in each aligned block of 4096 rows (0 to 4095, 4096 to 8191, ...) at most 256 rows name the same one
- cell: int32 [131072], P(('row', 'col')), may hold values from 0 to 129023
- near_list: int32 [1024, 4], P(('row', 'col')), may hold values from 0 to 31
- near_matrix: bfloat16 [1024, 4, 128, 128], P(('row', 'col')), may hold values from -0.25 to 0.25
- kernel_hat: float32 [1, 2048, 2048], P(None, ('row', 'col')), as said below
Outputs:
- forward_out: float32 [3, 131072], P(None, ('row', 'col'))
- adjoint_out: float32 [3, 131072], P(None, ('row', 'col'))
Inputs may be any that keep to these rules, and one draw needn't show every extreme that they name: Among the 4096 elements of one device no owner is named more than 256 times; in every draw some device names some owner exactly 256 times. Every entry is positive, and kernel_hat[t, ky, kx] equals kernel_hat[t, (2048 - ky) mod 2048, (2048 - kx) mod 2048].
All inputs are finite; a program needn't handle non-finite values.
Results may differ from a plain program's by a relative error of at most 0.0003.
Values sent between devices are 32-bit elements; how exact they have to be, the bound alone decides.
No kernel may reach another device: no remote copies, remote signals or barrier semaphores. Data moves between devices by JAX's collectives and lax.ppermute only.
A program may use at most 320 MiB of HBM per device.

v0:
```python
import math

import jax
import jax.numpy as jnp
import numpy as np
from jax import lax
from jax.experimental import pallas as pl
from jax.experimental.pallas import tpu as pltpu
from jax.sharding import PartitionSpec as P

AXES = ("row", "col")
LANES = 128
HALVES = 2
GROUP = 8
CHUNK = 1024
FIRST = 768
WINDOW = 256
F32 = jnp.float32
BF16 = jnp.bfloat16
NT = (((1,), (1,)), ((), ()))
NN = (((1,), (0,)), ((), ()))


def split_np(table):
    hi = table.astype(np.float32).astype(jnp.bfloat16)
    lo = (table - hi.astype(np.float64)).astype(np.float32).astype(jnp.bfloat16)
    return jnp.asarray(hi), jnp.asarray(lo)


def split(x):
    hi = x.astype(BF16)
    return hi, (x - hi.astype(F32)).astype(BF16)


def dot(a, b, dims):
    return lax.dot_general(a, b, dims, preferred_element_type=F32)


def dot3(a, b, dims):
    (ah, al), (bh, bl) = a, b
    return dot(ah, bh, dims) + (dot(ah, bl, dims) + dot(al, bh, dims))


def y_table(devices, per):
    d, c, h, q, hh, cc, y = np.ix_(
        range(devices), range(2), range(HALVES), range(per), range(HALVES), range(2), range(LANES)
    )
    angle = 2.0 * math.pi * (((d * per + q) * y) % LANES) / LANES
    sine = np.where(c < cc, 1.0, -1.0) * np.sin(angle)
    value = np.where(c == cc, np.cos(angle), sine) * (h == hh)
    return value.reshape(devices * 2 * HALVES * per, HALVES * 2 * LANES)


def x_table(length, direction):
    copies = LANES // length
    c, p, x, cc, pp, k = np.ix_(
        range(2), range(copies), range(length), range(2), range(copies), range(length)
    )
    angle = direction * 2.0 * math.pi * ((x * k) % length) / length
    sine = np.where(c < cc, 1.0, -1.0) * np.sin(angle)
    value = np.where(c == cc, np.cos(angle), sine) * (p == pp)
    return value.reshape(2 * LANES, 2 * LANES)


def phases(rows, cols, length):
    turns = (np.arange(rows)[:, None] * np.arange(cols)[None, :]) % length
    angle = 2.0 * math.pi * turns / length
    return np.cos(angle), np.sin(angle)


def fft_list(re, im, direction):
    n = len(re)
    if n == 1:
        return re, im
    even_re, even_im = fft_list(re[0::2], im[0::2], direction)
    odd_re, odd_im = fft_list(re[1::2], im[1::2], direction)
    low_re, low_im, high_re, high_im = [], [], [], []
    for k in range(n // 2):
        a, b = odd_re[k], odd_im[k]
        if k == 0:
            tr, ti = a, b
        elif 4 * k == n:
            tr, ti = (-b, a) if direction > 0 else (b, -a)
        else:
            cos = math.cos(2.0 * math.pi * k / n)
            sin = direction * math.sin(2.0 * math.pi * k / n)
            tr, ti = a * cos - b * sin, a * sin + b * cos
        low_re.append(even_re[k] + tr)
        low_im.append(even_im[k] + ti)
        high_re.append(even_re[k] - tr)
        high_im.append(even_im[k] - ti)
    return low_re + high_re, low_im + high_im


def one_hot(cols, start, size):
    ids = lax.broadcasted_iota(jnp.int32, (size, cols.shape[1]), 0) + start
    return jnp.where(ids == cols, 1.0, 0.0).astype(BF16)


def call(kernel, name, out_shape, args, scratch=(), smem_in=(), smem_out=(), far=(), flops=0, after=()):
    count, skip, results = len(args), len(after), len(out_shape)
    spaces = [
        pltpu.SMEM if i in smem_in else pl.ANY if i in far else pltpu.VMEM for i in range(count)
    ]
    outs = [pltpu.SMEM if i in smem_out else pltpu.VMEM for i in range(results)]
    moved = sum(math.prod(x.shape) * x.dtype.itemsize for x in (*args, *out_shape))
    near_by = [pltpu.VMEM(args[i].shape, args[i].dtype) for i in far]
    sems = [pltpu.SemaphoreType.DMA((len(far),))] if far else []

    def body(*refs):
        refs = refs[:count] + refs[count + skip :]
        if not far:
            return kernel(*refs)
        refs, targets, sem = list(refs[: -len(far) - 1]), refs[-len(far) - 1 : -1], refs[-1]
        copies = {}
        for j, i in enumerate(far):
            copies[i] = pltpu.make_async_copy(refs[i], targets[j], sem.at[j])
            copies[i].start()
            refs[i] = targets[j]

        def wait(*numbers):
            for i in numbers:
                copies[i].wait()

        return kernel(wait, *refs)

    return pl.pallas_call(
        body,
        out_shape=list(out_shape),
        in_specs=[pl.BlockSpec(memory_space=space) for space in spaces]
        + [pl.BlockSpec(memory_space=pl.ANY)] * skip,
        out_specs=[pl.BlockSpec(memory_space=space) for space in outs],
        scratch_shapes=[*scratch, *near_by, *sems],
        compiler_params=pltpu.CompilerParams(vmem_limit_bytes=32 << 20),
        cost_estimate=pl.CostEstimate(flops=flops, transcendentals=0, bytes_accessed=moved),
        name=name,
    )(*args, *after)


def shape(dims, dtype=F32):
    return jax.ShapeDtypeStruct(dims, dtype)


def expand_call(starts, keys, rows, devices, capacity, codes):
    count = keys.shape[1]
    wide = -(-capacity // LANES) * LANES + LANES
    height = 16

    def kernel(starts_ref, key_ref, *refs):
        row_refs, out_ref, s_ref = refs[:-2], refs[-2], refs[-1]
        s_ref[:, count:] = jnp.zeros((height, wide), F32)
        for i, ref in enumerate(row_refs):
            s_ref[i : i + 1, 0:count] = ref[...]
        s_ref[height - 1 : height, 0:count] = (key_ref[...] & (codes - 1)).astype(F32)
        lane = lax.broadcasted_iota(jnp.int32, (height, wide), 1)
        rank = lax.broadcasted_iota(jnp.int32, (height, wide), 0)
        free = jnp.where(rank == height - 1, -1.0, 0.0)

        @pl.loop(0, devices, unroll=4)
        def _(d):
            first = starts_ref[d]
            held = starts_ref[d + 1] - first
            tile = first // LANES
            block = s_ref[:, pl.ds(pl.multiple_of(tile * LANES, LANES), wide)]
            moved = pltpu.roll(block, wide - (first - tile * LANES), 1)
            kept = jnp.where(lane < held, moved, free)
            out_ref[d] = jnp.where(rank == height - 2, held.astype(F32), kept)[:, :capacity]

    (out,) = call(
        kernel,
        "expand",
        [shape((devices, height, capacity))],
        [starts, keys, *rows],
        scratch=[pltpu.VMEM((height, count + wide), F32)],
        smem_in=(0,),
    )
    return out


def compact_call(starts, data, count):
    devices, height, capacity = data.shape
    wide = -(-capacity // LANES) * LANES + LANES

    def kernel(starts_ref, in_ref, out_ref, s_ref, r_ref):
        lane = lax.broadcasted_iota(jnp.int32, (height, wide), 1)
        filler = jnp.zeros((height, wide - capacity), F32)

        @pl.loop(0, devices, unroll=4)
        def _(d):
            whole = jnp.concatenate([in_ref[d], filler], axis=1)
            r_ref[d] = pltpu.roll(whole, starts_ref[d] % LANES, 1)

        @pl.loop(0, devices)
        def _(d):
            first = starts_ref[d]
            shift = first % LANES
            left = pl.multiple_of(first - shift, LANES)
            edge = jnp.where(lane[:, :LANES] < shift, s_ref[:, pl.ds(left, LANES)], r_ref[d, :, :LANES])
            s_ref[:, pl.ds(left, LANES)] = edge
            s_ref[:, pl.ds(left + LANES, wide - LANES)] = r_ref[d, :, LANES:]

        out_ref[...] = s_ref[:, :count]

    (out,) = call(
        kernel,
        "compact",
        [shape((height, count))],
        [starts, data],
        scratch=[
            pltpu.VMEM((height, count + wide), F32),
            pltpu.VMEM((devices, height, wide), F32),
        ],
        smem_in=(0,),
    )
    return out


def turn_blocks(parts):
    parts = list(parts)
    block = lax.broadcasted_iota(jnp.int32, parts[0].shape, 1) // GROUP
    for m in (1, 2, 4, 8):
        high = (block & m) != 0
        for i in range(16):
            if i & m == 0:
                a, b = parts[i], parts[i + m]
                parts[i] = jnp.where(high, pltpu.roll(b, m * GROUP, 1), a)
                parts[i + m] = jnp.where(high, b, pltpu.roll(a, LANES - m * GROUP, 1))
    return parts


def pick_lanes(tiles, place):
    dims = tiles[0].shape
    index = jnp.broadcast_to(jnp.clip(place, 0.0, len(tiles) * LANES - 1.0).astype(jnp.int32), dims)
    result = None
    for k, tile in enumerate(tiles):
        part = jnp.take_along_axis(tile, index & (LANES - 1), axis=1)
        result = part if k == 0 else jnp.where(index < k * LANES, result, part)
    return result


def gather_groups(arrived, x_local, chunk):
    devices, height, capacity = arrived.shape
    slots = devices * capacity
    chunks = slots // chunk
    shift = x_local.bit_length() - 1
    none = 1 << 20

    def decode(code):
        return code & (x_local - 1), lax.shift_right_arithmetic(code, shift)

    if capacity % LANES or devices % 16:
        turned = arrived.reshape(devices, height, capacity // GROUP, GROUP)
        turned = jnp.transpose(turned, (1, 2, 0, 3)).reshape(height, slots)
        row, col = decode(turned[height - 1].astype(jnp.int32))
        per_chunk = col.reshape(chunks, chunk)
        low = jnp.min(jnp.where(per_chunk < 0, none, per_chunk), axis=1)
        bounds = jnp.stack([low, jnp.max(per_chunk, axis=1)])
        return turned, jnp.stack([row, col]), bounds, jnp.zeros((8, LANES), F32)

    tiles = capacity // LANES

    def kernel(in_ref, out_ref, rc_ref, bound_ref, held_ref):
        most = jnp.zeros((1, LANES), F32)
        for i in range(devices):
            held = in_ref[i, height - 2 : height - 1, :LANES]
            held_ref[i : i + 1] = held
            most = jnp.maximum(most, held)
        held_ref[devices:] = jnp.broadcast_to(most, (8, LANES))
        per = 1.0 / jnp.maximum(most, 1.0)
        lane = lax.broadcasted_iota(jnp.int32, (1, LANES), 1).astype(F32)
        rank = lax.broadcasted_iota(jnp.int32, (height, LANES), 0)
        free = jnp.where(rank == height - 1, -1.0, 0.0)

        @pl.loop(0, devices // 16 * tiles)
        def _(n):
            sb, t = n // tiles, n % tiles
            slot = lane + (t * LANES).astype(F32)
            parts = []
            for i in range(16):
                sender = sb * 16 + i
                held = in_ref[sender, height - 2 : height - 1, :LANES]
                place = jnp.floor((slot * held + 0.5) * per)
                before = jnp.floor(((slot - 1.0) * held + 0.5) * per)
                valid = (place > before) & (slot < most)
                across = [in_ref[sender, :, k * LANES : (k + 1) * LANES] for k in range(tiles)]
                parts.append(jnp.where(valid, pick_lanes(across, place), free))
            for j, part in enumerate(turn_blocks(parts)):
                left = (t * 16 + j) * devices * GROUP + sb * LANES
                at = pl.ds(pl.multiple_of(left, LANES), LANES)
                out_ref[:, at] = part
                row, col = decode(part[height - 1 :].astype(jnp.int32))
                rc_ref[0:1, at] = row
                rc_ref[1:2, at] = col

        @pl.loop(0, chunks)
        def _(i):
            col = rc_ref[1:2, pl.ds(pl.multiple_of(i * chunk, chunk), chunk)]
            bound_ref[0, i] = jnp.min(jnp.where(col < 0, none, col))
            bound_ref[1, i] = jnp.max(col)

    return call(
        kernel,
        "groups",
        [
            shape((height, slots)),
            shape((2, slots), jnp.int32),
            shape((2, chunks), jnp.int32),
            shape((devices + 8, LANES)),
        ],
        [arrived],
        smem_out=(2,),
    )


def scatter_groups(results, held, devices, capacity):
    height = results.shape[0]
    if capacity % LANES or devices % 16:
        turned = results.reshape(height, capacity // GROUP, devices, GROUP)
        return jnp.transpose(turned, (2, 0, 1, 3)).reshape(devices, height, capacity)

    tiles = capacity // LANES

    def kernel(in_ref, held_ref, out_ref):
        most = held_ref[devices : devices + 1]
        lane = lax.broadcasted_iota(jnp.int32, (1, LANES), 1).astype(F32)

        @pl.loop(0, devices // 16)
        def _(sb):
            turned = []
            for t in range(tiles):
                parts = []
                for j in range(16):
                    left = (t * 16 + j) * devices * GROUP
                    parts.append(in_ref[:, pl.ds(pl.multiple_of(left + sb * LANES, LANES), LANES)])
                turned.append(turn_blocks(parts))
            for i in range(16):
                sender = sb * 16 + i
                here = jnp.maximum(held_ref[pl.ds(sender, 1)], 1.0)
                for t in range(tiles):
                    place = jnp.floor(((lane + t * LANES) * most + here - 0.5) / here)
                    picked = pick_lanes([turned[k][i] for k in range(tiles)], place)
                    out_ref[sender, :, t * LANES : (t + 1) * LANES] = picked

    (out,) = call(kernel, "ungroup", [shape((devices, height, capacity))], [results, held])
    return out


def visit_windows(bound_ref, i, visit):
    first = pl.multiple_of(bound_ref[0, i] // LANES * LANES, LANES)
    visit(first, FIRST)

    def step(w, carry):
        visit(pl.multiple_of(first + FIRST + w * WINDOW, LANES), WINDOW)
        return carry

    lax.fori_loop(0, (bound_ref[1, i] - first - FIRST) // WINDOW + 1, step, 0)


def project_call(field, bounds, rc, payload, table, tw_cos, tw_sin, x_local, grid_y):
    slots = rc.shape[1]
    chunks = bounds.shape[1]
    chunk = slots // chunks
    n1 = grid_y // LANES
    k1l = n1 // HALVES
    rows = k1l * x_local
    width = HALVES * 2 * LANES
    half = 4 * x_local

    def kernel(wait, bound_ref, rc_ref, pay_ref, table_ref, cos_ref, sin_ref, out_ref, v_ref, acc_ref, x_ref):
        @pl.loop(0, half // 32)
        def _(i):
            acc_ref[pl.ds(pl.multiple_of(i * 64, 64), 64)] = jnp.zeros((64, acc_ref.shape[1]), F32)

        wait(1, 2)

        @pl.loop(0, chunks)
        def _(i):
            @pl.when(bound_ref[1, i] >= 0)
            def _():
                @pl.loop(0, chunk // 256)
                def _(j):
                    at = pl.ds(pl.multiple_of(i * chunk + j * 256, 256), 256)
                    to = pl.ds(pl.multiple_of(j * 256, 256), 256)
                    ids = lax.broadcasted_iota(jnp.int32, (x_local, 256), 0)
                    m0 = ids == rc_ref[0:1, at]
                    m1 = ids == rc_ref[0:1, at] + 1
                    for c in range(2):
                        u = pay_ref[3 * c + field : 3 * c + field + 1, at]
                        for b in range(2):
                            p0 = u * pay_ref[6 + 4 * c + b : 7 + 4 * c + b, at]
                            p1 = u * pay_ref[8 + 4 * c + b : 9 + 4 * c + b, at]
                            hi, lo = split(jnp.where(m0, p0, jnp.where(m1, p1, 0.0)))
                            base = (b * 2 + c) * x_local
                            v_ref[base : base + x_local, to] = hi
                            v_ref[half + base : half + base + x_local, to] = lo

                col = rc_ref[1:2, pl.ds(pl.multiple_of(i * chunk, chunk), chunk)]

                def visit(start, size):
                    acc_ref[:, pl.ds(start, size)] += dot(v_ref[...], one_hot(col, start, size), NT)

                visit_windows(bound_ref, i, visit)

        wait(3, 4, 5)

        @pl.loop(0, x_local // 8)
        def _(i):
            def rows_of(base):
                low = pl.ds(pl.multiple_of(base + i * 8, 8), 8)
                high = pl.ds(pl.multiple_of(half + base + i * 8, 8), 8)
                return acc_ref[low, :grid_y] + acc_ref[high, :grid_y]

            parts = []
            for c in range(2):
                g = rows_of(c * x_local) + pltpu.roll(rows_of((2 + c) * x_local), 1, 1)
                parts.append([g[:, y * LANES : (y + 1) * LANES] for y in range(n1)])
            re, im = fft_list(parts[0], parts[1], -1.0)
            for k in range(n1):
                cos, sin = cos_ref[k : k + 1, :], sin_ref[k : k + 1, :]
                to = pl.ds(pl.multiple_of((k % k1l) * x_local + i * 8, 8), 8)
                left = (k // k1l) * 2 * LANES
                x_ref[to, left : left + LANES] = re[k] * cos + im[k] * sin
                x_ref[to, left + LANES : left + 2 * LANES] = im[k] * cos - re[k] * sin

        part = min(rows, 256)

        @pl.loop(0, rows // part)
        def _(j):
            at = pl.ds(pl.multiple_of(j * part, part), part)
            out_ref[:, at] = dot3(split(table_ref[...]), split(x_ref[at]), NT)

    (out,) = call(
        kernel,
        "project",
        [shape((table.shape[0], rows))],
        [bounds, rc, payload, table, tw_cos, tw_sin],
        scratch=[
            pltpu.VMEM((2 * half, chunk), BF16),
            pltpu.VMEM((2 * half, grid_y + FIRST), F32),
            pltpu.VMEM((rows, width), F32),
        ],
        smem_in=(0,),
        far=(1, 2, 3, 4, 5),
        flops=4 * half * slots * grid_y,
    )
    return out


def spectral_call(data, kernel_t, fwd, inv, tw_cos, tw_sin, devices, after):
    lanes = data.shape[1]
    rows = data.shape[0] // (2 * devices)

    def kernel(wait, in_ref, kt_ref, fh_ref, fl_ref, ih_ref, il_ref, cos_ref, sin_ref, out_ref, re_ref, im_ref):
        wait(6, 7)

        @pl.loop(0, lanes // LANES)
        def _(t):
            at = pl.ds(pl.multiple_of(t * LANES, LANES), LANES)
            re = [in_ref[(2 * s) * rows : (2 * s + 1) * rows, at] for s in range(devices)]
            im = [in_ref[(2 * s + 1) * rows : (2 * s + 2) * rows, at] for s in range(devices)]
            re, im = fft_list(re, im, -1.0)
            for k in range(devices):
                cos, sin = cos_ref[k : k + 1, at], sin_ref[k : k + 1, at]
                re_ref[k * rows : (k + 1) * rows, at] = re[k] * cos + im[k] * sin
                im_ref[k * rows : (k + 1) * rows, at] = im[k] * cos - re[k] * sin

        wait(1, 2, 3, 4, 5)
        @pl.loop(0, lanes // LANES)
        def _(t):
            at = pl.ds(pl.multiple_of(t * LANES, LANES), LANES)
            both = jnp.concatenate([re_ref[:, at], im_ref[:, at]], axis=1)
            spectrum = dot3(split(both), (fh_ref[...], fl_ref[...]), NN)
            factor = kt_ref[:, at]
            both = jnp.concatenate([spectrum[:, :LANES] * factor, spectrum[:, LANES:] * factor], axis=1)
            back = dot3(split(both), (ih_ref[...], il_ref[...]), NN)
            re_ref[:, at] = back[:, :LANES]
            im_ref[:, at] = back[:, LANES:]

        @pl.loop(0, lanes // LANES)
        def _(t):
            at = pl.ds(pl.multiple_of(t * LANES, LANES), LANES)
            re, im = [], []
            for k in range(devices):
                cos, sin = cos_ref[k : k + 1, at], sin_ref[k : k + 1, at]
                a = re_ref[k * rows : (k + 1) * rows, at]
                b = im_ref[k * rows : (k + 1) * rows, at]
                re.append(a * cos - b * sin)
                im.append(b * cos + a * sin)
            re, im = fft_list(re, im, 1.0)
            for s in range(devices):
                out_ref[(2 * s) * rows : (2 * s + 1) * rows, at] = re[s]
                out_ref[(2 * s + 1) * rows : (2 * s + 2) * rows, at] = im[s]

    (out,) = call(
        kernel,
        "spectral",
        [shape(data.shape)],
        [data, kernel_t, *fwd, *inv, tw_cos, tw_sin],
        scratch=[
            pltpu.VMEM((devices * rows, lanes), F32),
            pltpu.VMEM((devices * rows, lanes), F32),
        ],
        far=(1, 2, 3, 4, 5, 6, 7),
        flops=1 << 30,
        after=after,
    )
    return out


def sample_call(data, bounds, rc, payload, table, tw_cos, tw_sin, x_local, grid_y, after):
    slots = rc.shape[1]
    n1 = grid_y // LANES
    k1l = n1 // HALVES
    rows = k1l * x_local
    width = HALVES * 2 * LANES
    chunks = bounds.shape[1]
    chunk = slots // chunks
    half = 4 * x_local

    def kernel(wait, in_ref, bound_ref, rc_ref, pay_ref, table_ref, cos_ref, sin_ref, out_ref, u_ref, g_ref, p_ref, t_ref):
        part = min(rows, 256)
        wait(4)

        @pl.loop(0, rows // part)
        def _(j):
            at = pl.ds(pl.multiple_of(j * part, part), part)
            u_ref[at] = dot3(split(jnp.transpose(in_ref[:, at])), split(table_ref[...]), NN)

        wait(5, 6)

        @pl.loop(0, x_local // 8)
        def _(i):
            re, im = [], []
            for k in range(n1):
                cos, sin = cos_ref[k : k + 1, :], sin_ref[k : k + 1, :]
                at = pl.ds(pl.multiple_of((k % k1l) * x_local + i * 8, 8), 8)
                left = (k // k1l) * 2 * LANES
                a = u_ref[at, left : left + LANES]
                b = u_ref[at, left + LANES : left + 2 * LANES]
                re.append(a * cos - b * sin)
                im.append(b * cos + a * sin)
            re, im = fft_list(re, im, 1.0)
            re_at = pl.ds(pl.multiple_of(i * 8, 8), 8)
            im_at = pl.ds(pl.multiple_of(x_local + i * 8, 8), 8)
            for y in range(n1):
                g_ref[re_at, y * LANES : (y + 1) * LANES] = re[y]
                g_ref[im_at, y * LANES : (y + 1) * LANES] = im[y]

        @pl.loop(0, x_local // 8)
        def _(i):
            at = pl.ds(pl.multiple_of(i * 16, 16), 16)
            for b in range(2):
                value = g_ref[at] if b == 0 else pltpu.roll(g_ref[at], grid_y - 1, 1)
                hi, lo = split(value)
                base = 2 * b * x_local
                p_ref[pl.ds(pl.multiple_of(base + i * 16, 16), 16), :grid_y] = hi
                p_ref[pl.ds(pl.multiple_of(half + base + i * 16, 16), 16), :grid_y] = lo

        p_ref[:, grid_y:] = jnp.zeros((2 * half, FIRST), BF16)
        out_ref[...] = jnp.zeros(out_ref.shape, F32)
        wait(2, 3)

        @pl.loop(0, chunks)
        def _(i):
            @pl.when(bound_ref[1, i] >= 0)
            def _():
                at = pl.ds(pl.multiple_of(i * chunk, chunk), chunk)

                col = rc_ref[1:2, at]

                def visit(start, size):
                    part = dot(p_ref[:, pl.ds(start, size)], one_hot(col, start, size), NN)
                    t_ref[...] = part if size == FIRST else t_ref[...] + part

                visit_windows(bound_ref, i, visit)
                @pl.loop(0, chunk // 256)
                def _(j):
                    at = pl.ds(pl.multiple_of(i * chunk + j * 256, 256), 256)
                    of = pl.ds(pl.multiple_of(j * 256, 256), 256)
                    ids = lax.broadcasted_iota(jnp.int32, (x_local, 256), 0)
                    m0 = ids == rc_ref[0:1, at]
                    m1 = ids == rc_ref[0:1, at] + 1
                    for c in range(2):
                        result = jnp.zeros((x_local, 256), F32)
                        for b in range(2):
                            other = 10 - 4 * c
                            w0 = pay_ref[other + b : other + b + 1, at]
                            w1 = pay_ref[other + 2 + b : other + 3 + b, at]
                            base = (b * 2 + c) * x_local
                            weight = jnp.where(m0, w0, jnp.where(m1, w1, 0.0))
                            low = t_ref[base : base + x_local, of]
                            high = t_ref[half + base : half + base + x_local, of]
                            result = result + weight * (low + high)
                        out_ref[c : c + 1, at] = jnp.sum(result, axis=0, keepdims=True)

    (out,) = call(
        kernel,
        "sample",
        [shape((2, slots))],
        [data, bounds, rc, payload, table, tw_cos, tw_sin],
        scratch=[
            pltpu.VMEM((rows, width), F32),
            pltpu.VMEM((2 * x_local, grid_y), F32),
            pltpu.VMEM((2 * half, grid_y + FIRST), BF16),
            pltpu.VMEM((2 * half, chunk), F32),
        ],
        smem_in=(1,),
        far=(2, 3, 4, 5, 6),
        flops=4 * half * slots * grid_y,
        after=after,
    )
    return out


def split_outside(x):
    hi = lax.reduce_precision(x, 8, 7)
    return hi.astype(BF16), (x - hi).astype(BF16)


def near_terms(currents, probes, near_list, near_matrix):
    block_len = near_matrix.shape[2]
    blocks = near_list.shape[0]
    select = (near_list[:, :, None] == jnp.arange(blocks, dtype=jnp.int32)[None, None, :]).astype(F32)
    cur_blocks = currents.reshape(3, blocks, block_len)
    gathered = jnp.einsum("ctj,bnt->cbnj", cur_blocks, select, precision=lax.Precision.HIGHEST)
    g_hi, g_lo = split_outside(gathered)
    forward = jnp.einsum(
        "cbnj,bnij->cbi", jnp.concatenate([g_hi, g_lo]), near_matrix, preferred_element_type=F32
    )
    p_hi, p_lo = split_outside(probes.reshape(3, blocks, block_len))
    spread = jnp.einsum(
        "cbi,bnij->cbnj", jnp.concatenate([p_hi, p_lo]), near_matrix, preferred_element_type=F32
    )
    adjoint = jnp.einsum(
        "cbnj,bnt->ctj", spread[:3] + spread[3:], select, precision=lax.Precision.HIGHEST
    )
    return (forward[:3] + forward[3:]).reshape(3, -1), adjoint.reshape(3, -1)


def on_device(
    currents, probes, proj_weights, interp_weights, owner, cell, near_list, near_matrix, kernel_hat
):
    devices = lax.axis_size("row") * lax.axis_size("col")
    elem_count = currents.shape[1]
    capacity = 2 * elem_count // devices
    dz_count, ky_local, grid_x = kernel_hat.shape
    assert dz_count == 1
    grid_y = ky_local * devices
    x_local = grid_x // devices
    slots = devices * capacity
    n1 = grid_y // LANES
    per = ky_local // n1
    k1l = n1 // HALVES

    codes = x_local * grid_y
    assert codes & (codes - 1) == 0

    target = owner[:, 0]
    row, col = cell // grid_y % (x_local - 1), cell % grid_y
    key = target * codes + col * x_local + row
    columns = [*currents, *probes, *proj_weights, *interp_weights]
    order = lax.iota(jnp.int32, elem_count)
    key, *columns, order = lax.sort((key, *columns, order), num_keys=1, is_stable=False)
    bounds_of = jnp.arange(devices + 1, dtype=jnp.int32)
    starts = jnp.sum((target[None, :] < bounds_of[:, None]).astype(jnp.int32), axis=1)
    outgoing = expand_call(
        starts, key[None, :], [x[None, :] for x in columns], devices, capacity, codes
    )
    arrived = lax.all_to_all(outgoing, AXES, split_axis=0, concat_axis=0, tiled=True)
    payload, rc, bounds, held = gather_groups(arrived, x_local, CHUNK)

    table = jnp.asarray(y_table(devices, per), F32)
    ty_cos, ty_sin = (jnp.asarray(t, F32) for t in phases(n1, LANES, grid_y))
    tx_cos, tx_sin = (
        jnp.asarray(np.tile(t, (1, k1l)), F32) for t in phases(devices, x_local, grid_x)
    )
    fwd, inv = split_np(x_table(x_local, -1.0)), split_np(x_table(x_local, 1.0))

    kernel_view = kernel_hat.reshape(per, HALVES, k1l, x_local, devices)
    kernel_t = jnp.transpose(kernel_view, (4, 1, 0, 2, 3)) * (1.0 / (grid_x * grid_y))
    kernel_t = kernel_t.reshape(devices * HALVES * per, k1l * x_local)

    def exchange(*fields):
        shaped = [x.reshape(devices, -1, x.shape[1]) for x in fields]
        height = shaped[0].shape[1]
        moved = lax.all_to_all(
            jnp.concatenate(shaped, axis=1), AXES, split_axis=0, concat_axis=0, tiled=True
        )
        parts = [moved[:, i * height : (i + 1) * height] for i in range(len(fields))]
        return [x.reshape(fields[0].shape) for x in parts]

    def spectral(spectra, *after):
        return spectral_call(spectra, kernel_t, fwd, inv, tx_cos, tx_sin, devices, after)

    def sample(products, *after):
        return sample_call(
            products, bounds, rc, payload, table, ty_cos, ty_sin, x_local, grid_y, after
        )

    spectra = []
    for field in range(3):
        grids = project_call(field, bounds, rc, payload, table, ty_cos, ty_sin, x_local, grid_y)
        spectra.extend(exchange(grids))
    products = exchange(spectral(spectra[0]), spectral(spectra[1]))
    products += exchange(spectral(spectra[2]))
    first = sample(products[0])
    second = sample(products[1])
    third = sample(products[2], first, second)
    results = [first, second, third]
    returning = scatter_groups(jnp.concatenate(results, axis=0), held, devices, capacity)
    returned = lax.all_to_all(returning, AXES, split_axis=0, concat_axis=0, tiled=True)
    homed = compact_call(starts, returned, elem_count)
    _, *homed = lax.sort((order, *homed), num_keys=1, is_stable=False)
    near_forward, near_adjoint = near_terms(currents, probes, near_list, near_matrix)
    return (jnp.stack(homed[0::2]) + near_forward, jnp.stack(homed[1::2]) + near_adjoint)


def solution(mesh):
    return jax.shard_map(
        on_device,
        mesh=mesh,
        in_specs=(
            P(None, AXES),
            P(None, AXES),
            P(None, AXES),
            P(None, AXES),
            P(AXES, None),
            P(AXES),
            P(AXES, None),
            P(AXES, None, None, None),
            P(None, AXES, None),
        ),
        out_specs=(P(None, AXES), P(None, AXES)),
        check_vma=False,
    )
```

profile of v0, /device:TPU:0, one launch (start us, length us, event | category | flops | bytes accessed | tf_op | source)
XLA Modules:
  0.0 278.1 jit_solution(15325053110702485153)
XLA Ops:
  0.6 1.1 fusion.26
  1.7 1.1 fusion.25
  2.8 1.0 fusion.28
  3.8 1.0 fusion.27
  4.8 0.9 convert_reduce_fusion.refs_0_
  5.7 0.8 fusion.18
  6.4 5.4 %sort.144 = (s32[4096]{0:T(1024)S(1)}, f32[4096]{0:T(1024)S(1)}, f32[4096]{0:T(1024)S(1)}, f32[4096]{0:T(1024)S(1)}, f32[4096]{0:T(1024)S(1)}, /*index=5*/f32[40...) sort(s32[4096]{0:T(1024)S(1)} %fusion.18, ...), dimensions={0}, to_apply=%region_0.1 | sort | flops 49152 | bytes 524288 | tf_op jit(solution)/shard_map/sort | solution.py:663
  11.8 1.5 expand.1
  13.3 23.5 %all_to_all.35.refs_0_ = f32[32,16,256]{2,1,0:T(8,128)S(1)} all-to-all(f32[32,16,256]{2,1,0:T(8,128)S(1)} %expand.1), channel_id=1, replica_groups=mesh['row'=4,'col'=8] {'row','col'}, dimensions={0} | all-to-all | bytes 1048576 | tf_op jit(solution)/shard_map/all_to_all | solution.py:669
  36.8 4.3 %groups.1 = (f32[16,8192]{1,0:T(8,128)S(1)}, s32[2,8192]{1,0:T(2,128)S(1)}, s32[2,8]{1,0:T(2,128)S(1)}, f32[40,128]{1,0:T(8,128)S(1)}) custom-call(f32[32,16,256]{2,1,0:T(8,128)S(1)} %all_to_all.35.refs_0_), custom_call_target="tpu_custom_call" | custom-call | bytes 1134656 | tf_op jit(solution)/shard_map/groups/pallas_call | solution.py:127
  41.1 0.0 copy-start.5
  41.1 1.4 copy-done.5
  42.5 0.7 copy-done.19
  43.2 0.7 copy-done.21
  43.9 11.3 %project.3 = f32[512,512]{1,0:T(8,128)} custom-call(s32[2,8]{1,0:T(2,128)S(1)} %get-tuple-element.44.refs_0_.refs_1_, s32[2,8192]{1,0:T(2,128)S(1)} %get-tuple-element.45.refs_1_.refs_2_, f32[16,8192]{1,0:T(8,128)S(1)} %get-tuple-element.46.refs_2_.refs_3_, f32[512,512]{1,0:T(8,128)S(1)} %copy-done.5, f32[16,128]{1,0:T(8,128)S(1)} %copy-done.19, ...), custom_call_target="tpu_custom_call" | custom-call | flops 17179869184 | bytes 2703424 | tf_op jit(solution)/shard_map/project/pallas_call | solution.py:127
  55.3 5.9 %all-to-all-start.1 = ((f32[32,16,512]{2,1,0:T(8,128)}), f32[32,16,512]{2,1,0:T(8,128)S(1)}, u32[]{:S(2)}, u32[]{:S(2)}) async-start(f32[32,16,512]{2,1,0:T(8,128)} %bitcast.30), calls=%async_computation.1 | async-start | bytes 2097152 | tf_op jit(solution)/shard_map/all_to_all | solution.py:686
  61.2 11.3 %project.4 = f32[512,512]{1,0:T(8,128)} custom-call(s32[2,8]{1,0:T(2,128)S(1)} %get-tuple-element.44.refs_0_.refs_1_, s32[2,8192]{1,0:T(2,128)S(1)} %get-tuple-element.45.refs_1_.refs_2_, f32[16,8192]{1,0:T(8,128)S(1)} %get-tuple-element.46.refs_2_.refs_3_, f32[512,512]{1,0:T(8,128)S(1)} %copy-done.6, f32[16,128]{1,0:T(8,128)S(1)} %copy-done.20, ...), custom_call_target="tpu_custom_call" | custom-call | flops 17179869184 | bytes 2703424 | tf_op jit(solution)/shard_map/project/pallas_call | solution.py:127
  72.5 16.3 %all-to-all-done.1 = f32[32,16,512]{2,1,0:T(8,128)S(1)} async-done(((f32[32,16,512]{2,1,0:T(8,128)}), f32[32,16,512]{2,1,0:T(8,128)S(1)}, u32[]{:S(2)}, u32[]{:S(2)}) %all-to-all-start.1) | async-done | bytes 1048608 | tf_op jit(solution)/shard_map/all_to_all | solution.py:686
  88.8 2.8 %all-to-all-start.2 = ((f32[32,16,512]{2,1,0:T(8,128)}), f32[32,16,512]{2,1,0:T(8,128)S(1)}, u32[]{:S(2)}, u32[]{:S(2)}) async-start(f32[32,16,512]{2,1,0:T(8,128)} %bitcast.34), calls=%async_computation.2 | async-start | bytes 2097152 | tf_op jit(solution)/shard_map/all_to_all | solution.py:686
  91.6 1.2 copy-done.7
  92.9 10.3 %project.5 = f32[512,512]{1,0:T(8,128)S(1)} custom-call(s32[2,8]{1,0:T(2,128)S(1)} %get-tuple-element.44.refs_0_.refs_1_, s32[2,8192]{1,0:T(2,128)S(1)} %get-tuple-element.45.refs_1_.refs_2_, f32[16,8192]{1,0:T(8,128)S(1)} %get-tuple-element.46.refs_2_.refs_3_, f32[512,512]{1,0:T(8,128)S(1)} %copy-done.7, f32[16,128]{1,0:T(8,128)S(1)} %copy-done.20, ...), custom_call_target="tpu_custom_call" | custom-call | flops 17179869184 | bytes 2703424 | tf_op jit(solution)/shard_map/project/pallas_call | solution.py:127
  103.2 1.0 copy-done
  104.2 14.8 %all-to-all-done.2 = f32[32,16,512]{2,1,0:T(8,128)S(1)} async-done(((f32[32,16,512]{2,1,0:T(8,128)}), f32[32,16,512]{2,1,0:T(8,128)S(1)}, u32[]{:S(2)}, u32[]{:S(2)}) %all-to-all-start.2) | async-done | bytes 1048608 | tf_op jit(solution)/shard_map/all_to_all | solution.py:686
  119.0 2.6 all-to-all-start.4
  121.7 0.0 copy-start.10
  121.7 1.9 broadcast_multiply_fusion
  123.6 3.0 %mul.30 = f32[4,2,8,64,32]{4,3,2,1,0:T(8,128)} reshape(f32[1,64,2048]{2,1,0:T(8,128)} %broadcast_multiply_fusion) | data formatting | bytes 1048576 | tf_op jit(solution)/shard_map/mul | solution.py:680
  126.6 3.3 %copy.28 = f32[32,2,4,8,64]{4,3,2,1,0:T(8,128)} copy(f32[32,2,4,8,64]{0,4,3,1,2:T(8,128)} %bitcast.130) | data formatting | bytes 1048576 | tf_op jit(solution)/shard_map/mul | solution.py:680
  129.9 2.3 reshape.62.refs_1_
  132.2 1.0 copy-done.1
  133.3 0.9 copy-done.11
  134.2 0.9 copy-done.13
  135.1 0.8 copy-done.15
  135.9 0.8 copy-done.17
  136.8 4.5 %spectral.3 = f32[512,512]{1,0:T(8,128)S(1)} custom-call(f32[512,512]{1,0:T(8,128)S(1)} %bitcast.107, f32[256,512]{1,0:T(8,128)S(1)} %copy-done.1, bf16[256,256]{1,0:T(8,128)(2,1)S(1)} %copy-done.9, bf16[256,256]{1,0:T(8,128)(2,1)S(1)} %copy-done.10, bf16[256,256]{1,0:T(8,128)(2,1)S(1)} %copy-done.11, bf16[256,256]{1,0:T(8,128)(2,1)S(1)} %copy-done.13, ...), custom_call_target="tpu_custom_call" | custom-call | flops 1073741824 | bytes 3276800 | tf_op jit(solution)/shard_map/spectral/pallas_call | solution.py:127
  141.2 4.5 %spectral.4 = f32[512,512]{1,0:T(8,128)S(1)} custom-call(f32[512,512]{1,0:T(8,128)S(1)} %bitcast.108, f32[256,512]{1,0:T(8,128)S(1)} %copy-done.1, bf16[256,256]{1,0:T(8,128)(2,1)S(1)} %copy-done.9, bf16[256,256]{1,0:T(8,128)(2,1)S(1)} %copy-done.10, bf16[256,256]{1,0:T(8,128)(2,1)S(1)} %copy-done.11, bf16[256,256]{1,0:T(8,128)(2,1)S(1)} %copy-done.13, ...), custom_call_target="tpu_custom_call" | custom-call | flops 1073741824 | bytes 3276800 | tf_op jit(solution)/shard_map/spectral/pallas_call | solution.py:127
  145.8 1.6 pad_maximum_fusion
  147.4 1.9 all-to-all-done.4
  149.3 4.1 %all-to-all-start.3 = ((f32[32,32,512]{2,1,0:T(8,128)}), f32[32,32,512]{2,1,0:T(8,128)}, u32[]{:S(2)}, u32[]{:S(2)}) async-start(f32[32,32,512]{2,1,0:T(8,128)} %pad_maximum_fusion), calls=%async_computation.3 | async-start | bytes 4194304 | tf_op jit(solution)/shard_map/all_to_all | solution.py:686
  153.4 2.8 %convolution_bitcast_fusion = f32[6,32,4,128]{3,0,2,1:T(8,128)S(1)} fusion(bf16[32,4,128,128]{3,2,1,0:T(8,128)(2,1)} %param.25, bf16[3,32,128]{2,0,1:T(4,128)(2,1)S(1)} %get-tuple-element.65, bf16[3,32,128]{2,0,1:T(4,128)(2,1)S(1)} %get-tuple-element.64), kind=kOutput, calls=%fused_computation.1 | convolution fusion | flops 25264128 | bytes 4636672 | tf_op jit(solution)/shard_map/cbi,bnij->cbnj/dot_general | solution.py:631
  156.3 0.1 slice_add_fusion
  156.4 0.9 convolution_bitcast_fusion.3
  157.2 1.0 reduce-precision_convert_fusion
  158.2 0.9 copy-done.12
  159.1 0.9 copy-done.14
  160.1 0.8 copy-done.16
  160.9 0.8 copy-done.18
  161.7 5.5 %spectral.5 = f32[512,512]{1,0:T(8,128)} custom-call(f32[512,512]{1,0:T(8,128)S(1)} %bitcast.106, f32[256,512]{1,0:T(8,128)S(1)} %copy-done.2, bf16[256,256]{1,0:T(8,128)(2,1)S(1)} %copy-done.9, bf16[256,256]{1,0:T(8,128)(2,1)S(1)} %copy-done.10, bf16[256,256]{1,0:T(8,128)(2,1)S(1)} %copy-done.12, bf16[256,256]{1,0:T(8,128)(2,1)S(1)} %copy-done.14, ...), custom_call_target="tpu_custom_call" | custom-call | flops 1073741824 | bytes 3276800 | tf_op jit(solution)/shard_map/spectral/pallas_call | solution.py:127
  167.2 36.2 %all-to-all-done.3 = f32[32,32,512]{2,1,0:T(8,128)} async-done(((f32[32,32,512]{2,1,0:T(8,128)}), f32[32,32,512]{2,1,0:T(8,128)}, u32[]{:S(2)}, u32[]{:S(2)}) %all-to-all-start.3) | async-done | bytes 2097184 | tf_op jit(solution)/shard_map/all_to_all | solution.py:686
  203.4 2.9 %all-to-all-start.5 = ((f32[32,16,512]{2,1,0:T(8,128)}), f32[32,16,512]{2,1,0:T(8,128)S(1)}, u32[]{:S(2)}, u32[]{:S(2)}) async-start(f32[32,16,512]{2,1,0:T(8,128)} %bitcast.41), calls=%async_computation.5 | async-start | bytes 2097152 | tf_op jit(solution)/shard_map/all_to_all | solution.py:686
  206.3 1.9 fusion.23
  208.2 10.4 %sample.4.refs_8_ = f32[2,8192]{1,0:T(2,128)S(1)} custom-call(f32[512,512]{1,0:T(8,128)S(1)} %bitcast.113, s32[2,8]{1,0:T(2,128)S(1)} %get-tuple-element.44.refs_0_.refs_1_, s32[2,8192]{1,0:T(2,128)S(1)} %get-tuple-element.45.refs_1_.refs_2_, f32[16,8192]{1,0:T(8,128)S(1)} %copy-done.4, f32[512,512]{1,0:T(8,128)S(1)} %copy-done.8, f32[16,128]{1,0:T(8,128)S(1)} %copy-done.20, ...), custom_call_target="tpu_custom_call" | custom-call | flops 17179869184 | bytes 2768960 | tf_op jit(solution)/shard_map/sample/pallas_call | solution.py:127
  218.7 10.4 %sample.3.refs_7_ = f32[2,8192]{1,0:T(2,128)S(1)} custom-call(f32[512,512]{1,0:T(8,128)S(1)} %bitcast.111, s32[2,8]{1,0:T(2,128)S(1)} %get-tuple-element.44.refs_0_.refs_1_, s32[2,8192]{1,0:T(2,128)S(1)} %get-tuple-element.45.refs_1_.refs_2_, f32[16,8192]{1,0:T(8,128)S(1)} %copy-done.4, f32[512,512]{1,0:T(8,128)S(1)} %copy-done.8, f32[16,128]{1,0:T(8,128)S(1)} %copy-done.20, ...), custom_call_target="tpu_custom_call" | custom-call | flops 17179869184 | bytes 2768960 | tf_op jit(solution)/shard_map/sample/pallas_call | solution.py:127
  229.1 4.6 %all-to-all-done.5 = f32[32,16,512]{2,1,0:T(8,128)S(1)} async-done(((f32[32,16,512]{2,1,0:T(8,128)}), f32[32,16,512]{2,1,0:T(8,128)S(1)}, u32[]{:S(2)}, u32[]{:S(2)}) %all-to-all-start.5) | async-done | bytes 1048608 | tf_op jit(solution)/shard_map/all_to_all | solution.py:686
  233.7 10.4 %sample.5 = f32[2,8192]{1,0:T(2,128)S(1)} custom-call(f32[512,512]{1,0:T(8,128)S(1)} %bitcast.109, s32[2,8]{1,0:T(2,128)S(1)} %get-tuple-element.44.refs_0_.refs_1_, s32[2,8192]{1,0:T(2,128)S(1)} %get-tuple-element.45.refs_1_.refs_2_, f32[16,8192]{1,0:T(8,128)S(1)} %copy-done.4, f32[512,512]{1,0:T(8,128)S(1)} %copy-done.8, f32[16,128]{1,0:T(8,128)S(1)} %copy-done.20, ...), custom_call_target="tpu_custom_call" | custom-call | flops 17179869184 | bytes 2768960 | tf_op jit(solution)/shard_map/sample/pallas_call | solution.py:127
  244.1 0.1 pad_maximum_fusion.1.refs_0_
  244.2 1.7 ungroup.1
  246.0 13.3 %all-to-all-start.6 = ((f32[32,6,256]{2,1,0:T(8,128)}), f32[32,6,256]{2,1,0:T(8,128)S(1)}, u32[]{:S(2)}, u32[]{:S(2)}) async-start(f32[32,6,256]{2,1,0:T(8,128)} %ungroup.1), calls=%async_computation.6 | async-start | bytes 524288 | tf_op jit(solution)/shard_map/all_to_all | solution.py:711
  259.4 3.4 %convolution_bitcast_fusion.2 = f32[6,32,128]{2,0,1:T(8,128)S(1)} fusion(bf16[32,4,128,128]{3,2,1,0:T(8,128)(2,1)} %param.25, bf16[6,32,4,128]{3,1,0,2:T(8,128)(2,1)S(1)} %pad_maximum_fusion.2), kind=kOutput, calls=%fused_computation.3 | convolution fusion | flops 25165824 | bytes 4489216 | tf_op jit(solution)/shard_map/cbnj,bnij->cbi/dot_general | solution.py:627
  262.7 7.2 %all-to-all-done.6.refs_1_ = f32[32,6,256]{2,1,0:T(8,128)S(1)} async-done(((f32[32,6,256]{2,1,0:T(8,128)}), f32[32,6,256]{2,1,0:T(8,128)S(1)}, u32[]{:S(2)}, u32[]{:S(2)}) %all-to-all-start.6) | async-done | bytes 196640 | tf_op jit(solution)/shard_map/all_to_all | solution.py:711
  270.0 1.7 compact.1
  271.7 0.1 fusion.24
  271.7 5.6 %sort.145 = (s32[4096]{0:T(1024)}, f32[4096]{0:T(1024)S(1)}, f32[4096]{0:T(1024)S(1)}, f32[4096]{0:T(1024)S(1)}, f32[4096]{0:T(1024)S(1)}, /*index=5*/f32[4096]{0:T(1024)S(1)}, f32[4096]{0:T(1024)S(1)}) sort(s32[4096]{0:T(1024)S(1)} %get-tuple-element.28, f32[4096]{0:T(1024)S(1)} %bitcast.137, f32[4096]{0:T(1024)S(1)} %bitcast.136, f32[4096]{0:T(1024)S(1)} %bitcast.135, ...), dimensions={0}, to_apply=%region_2.3 | sort | flops 49152 | bytes 229376 | tf_op jit(solution)/shard_map/sort | solution.py:713
  277.4 0.8 bitcast_add_fusion
  (45 shorter events, 0.1 us)
Async XLA Ops:
  41.1 50.5 %copy-start.3 = (f32[16,8192]{1,0:T(8,128)}, f32[16,8192]{1,0:T(8,128)S(1)}, u32[]{:S(2)}) copy-start(f32[16,8192]{1,0:T(8,128)S(1)} %get-tuple-element.46.refs_2_.refs_3_) | copy-start | bytes 1572868
  41.1 1.4 copy-start.5
  42.5 0.7 copy-start.19
  43.2 0.7 copy-start.21
  43.9 17.3 %copy-start.6 = (f32[512,512]{1,0:T(8,128)S(1)}, f32[512,512]{1,0:T(8,128)}, u32[]{:S(2)}) copy-start(f32[512,512]{1,0:T(8,128)} %constant.61.clone.refs_3_.refs_4_) | copy-start | bytes 3145732
  43.9 17.3 %copy-start.20 = (f32[16,128]{1,0:T(8,128)S(1)}, f32[16,128]{1,0:T(8,128)}, u32[]{:S(2)}) copy-start(f32[16,128]{1,0:T(8,128)} %constant.62.clone.refs_4_.refs_5_) | copy-start | bytes 24580
  55.3 33.5 %all-to-all-start.1 = ((f32[32,16,512]{2,1,0:T(8,128)}), f32[32,16,512]{2,1,0:T(8,128)S(1)}, u32[]{:S(2)}, u32[]{:S(2)}) async-start(f32[32,16,512]{2,1,0:T(8,128)} %bitcast.30), calls=%async_computation.1 | async-start | bytes 2097152 | tf_op jit(solution)/shard_map/all_to_all | solution.py:686
  88.8 30.2 %all-to-all-start.2 = ((f32[32,16,512]{2,1,0:T(8,128)}), f32[32,16,512]{2,1,0:T(8,128)S(1)}, u32[]{:S(2)}, u32[]{:S(2)}) async-start(f32[32,16,512]{2,1,0:T(8,128)} %bitcast.34), calls=%async_computation.2 | async-start | bytes 2097152 | tf_op jit(solution)/shard_map/all_to_all | solution.py:686
  91.6 1.2 copy-start.7
  103.2 1.0 copy-start
  119.0 30.2 %all-to-all-start.4 = ((f32[32,16,512]{2,1,0:T(8,128)}), f32[32,16,512]{2,1,0:T(8,128)S(1)}, u32[]{:S(2)}, u32[]{:S(2)}) async-start(f32[32,16,512]{2,1,0:T(8,128)} %bitcast.110), calls=%async_computation.4 | async-start | bytes 2097152 | tf_op jit(solution)/shard_map/all_to_all | solution.py:686
  121.7 10.5 %copy-start.9 = (bf16[256,256]{1,0:T(8,128)(2,1)S(1)}, bf16[256,256]{1,0:T(8,128)(2,1)}, u32[]{:S(2)}) copy-start(bf16[256,256]{1,0:T(8,128)(2,1)} %constant.66.clone.refs_2_) | copy-start | bytes 393220
  121.7 10.5 %copy-start.10 = (bf16[256,256]{1,0:T(8,128)(2,1)S(1)}, bf16[256,256]{1,0:T(8,128)(2,1)}, u32[]{:S(2)}) copy-start(bf16[256,256]{1,0:T(8,128)(2,1)} %constant.67.clone.refs_3_) | copy-start | bytes 393220
  132.2 1.0 copy-start.1
  133.3 0.9 copy-start.11
  134.2 0.9 copy-start.13
  135.1 0.8 copy-start.15
  135.9 0.8 copy-start.17
  145.8 7.6 %copy-start.25 = (f32[3,4096]{1,0:T(4,128)S(1)}, f32[3,4096]{1,0:T(4,128)}, u32[]{:S(2)}) copy-start(f32[3,4096]{1,0:T(4,128)} %param.19) | copy-start | bytes 147460
  147.4 9.0 %copy-start.28 = (s32[32,4]{0,1:T(4,128)S(1)}, s32[32,4]{0,1:T(4,128)}, u32[]{:S(2)}) copy-start(s32[32,4]{0,1:T(4,128)} %param.24) | copy-start | bytes 1540
  147.4 9.9 %copy-start.27 = (f32[3,4096]{1,0:T(4,128)S(1)}, f32[3,4096]{1,0:T(4,128)}, u32[]{:S(2)}) copy-start(f32[3,4096]{1,0:T(4,128)} %param.18) | copy-start | bytes 147460
  147.4 10.8 %copy-start.2 = (f32[256,512]{1,0:T(8,128)S(1)}, f32[256,512]{1,0:T(8,128)}, u32[]{:S(2)}) copy-start(f32[256,512]{1,0:T(8,128)} %reshape.62.refs_1_) | copy-start | bytes 1572868
  149.3 54.2 %all-to-all-start.3 = ((f32[32,32,512]{2,1,0:T(8,128)}), f32[32,32,512]{2,1,0:T(8,128)}, u32[]{:S(2)}, u32[]{:S(2)}) async-start(f32[32,32,512]{2,1,0:T(8,128)} %pad_maximum_fusion), calls=%async_computation.3 | async-start | bytes 4194304 | tf_op jit(solution)/shard_map/all_to_all | solution.py:686
  158.2 0.9 copy-start.12
  159.1 0.9 copy-start.14
  160.1 0.8 copy-start.16
  160.9 0.8 copy-start.18
  161.7 46.4 %copy-start.4 = (f32[16,8192]{1,0:T(8,128)S(1)}, f32[16,8192]{1,0:T(8,128)}, u32[]{:S(2)}) copy-start(f32[16,8192]{1,0:T(8,128)} %copy-done.3) | copy-start | bytes 1572868
  161.7 46.5 %copy-start.8 = (f32[512,512]{1,0:T(8,128)S(1)}, f32[512,512]{1,0:T(8,128)}, u32[]{:S(2)}) copy-start(f32[512,512]{1,0:T(8,128)} %constant.61.clone.refs_3_.refs_4_) | copy-start | bytes 3145732
  161.7 46.5 %copy-start.22 = (f32[16,128]{1,0:T(8,128)S(1)}, f32[16,128]{1,0:T(8,128)}, u32[]{:S(2)}) copy-start(f32[16,128]{1,0:T(8,128)} %constant.63.clone.refs_5_.refs_6_) | copy-start | bytes 24580
  203.4 30.2 %all-to-all-start.5 = ((f32[32,16,512]{2,1,0:T(8,128)}), f32[32,16,512]{2,1,0:T(8,128)S(1)}, u32[]{:S(2)}, u32[]{:S(2)}) async-start(f32[32,16,512]{2,1,0:T(8,128)} %bitcast.41), calls=%async_computation.5 | async-start | bytes 2097152 | tf_op jit(solution)/shard_map/all_to_all | solution.py:686
  233.7 25.6 %copy-start.23 = (bf16[3,32,4,128]{3,1,0,2:T(8,128)(2,1)S(1)}, bf16[3,32,4,128]{3,1,0,2:T(8,128)(2,1)}, u32[]{:S(2)}) copy-start(bf16[3,32,4,128]{3,1,0,2:T(8,128)(2,1)} %get-tuple-element.56) | copy-start | bytes 294916
  233.7 25.6 %copy-start.24 = (bf16[3,32,4,128]{3,1,0,2:T(8,128)(2,1)S(1)}, bf16[3,32,4,128]{3,1,0,2:T(8,128)(2,1)}, u32[]{:S(2)}) copy-start(bf16[3,32,4,128]{3,1,0,2:T(8,128)(2,1)} %get-tuple-element.57) | copy-start | bytes 294916
  244.1 33.2 %copy-start.26 = (f32[1,3,32,128]{3,2,1,0:T(8,128)S(1)}, f32[1,3,32,128]{3,2,1,0:T(8,128)}, u32[]{:S(2)}) copy-start(f32[1,3,32,128]{3,2,1,0:T(8,128)} %convolution_bitcast_fusion.3) | copy-start | bytes 147460
  246.0 24.0 %all-to-all-start.6 = ((f32[32,6,256]{2,1,0:T(8,128)}), f32[32,6,256]{2,1,0:T(8,128)S(1)}, u32[]{:S(2)}, u32[]{:S(2)}) async-start(f32[32,6,256]{2,1,0:T(8,128)} %ungroup.1), calls=%async_computation.6 | async-start | bytes 524288 | tf_op jit(solution)/shard_map/all_to_all | solution.py:711
where the time goes:
time: 279 us; the launch traced here: 278 us
  Pallas kernels  88 us (32%)
  waiting for transfers between devices  81 us (29%)
  starting transfers between devices  31.6 us (11%)
  local copies, waits for them, and re-layouts  27.7 us (10%)
  blocking collectives  23.5 us (8%)
  other arithmetic  17.2 us (6%)
  matrix products  8.11 us (3%)
    pallas_call x13, Pallas kernels, call(): pl.pallas_call(body, out_shape=list(out_shape), in_specs=[pl.BlockSpec(me...  88 us
    all_to_all x5, waiting for transfers between devices, exchange(): lax.all_to_all(jnp.concatenate(shaped, axis=1), AXES, split_axis=0, conca...  73.8 us
    all_to_all x1, blocking collectives, on_device(): lax.all_to_all(outgoing, AXES, split_axis=0, concat_axis=0, tiled=True)  23.5 us
    all_to_all x5, starting transfers between devices, exchange(): lax.all_to_all(jnp.concatenate(shaped, axis=1), AXES, split_axis=0, conca...  18.3 us
    all_to_all x1, starting transfers between devices, on_device(): lax.all_to_all(returning, AXES, split_axis=0, concat_axis=0, tiled=True)  13.3 us
    unnamed x58, local copies, waits for them, and re-layouts  13.1 us
    all_to_all x1, waiting for transfers between devices, on_device(): lax.all_to_all(returning, AXES, split_axis=0, concat_axis=0, tiled=True)  7.21 us
    mul x2, local copies, waits for them, and re-layouts, on_device(): jnp.transpose(kernel_view, (4, 1, 0, 2, 3)) * (1.0 / (grid_x * grid_y))  6.3 us
  transfers between devices with their start and end apart: 6, of which 6 were waited for; matrix products, arithmetic and copies ran while one was open for 8% of the time, Pallas kernels for 20%

commit v1 on v0

--- a/solution.py
+++ b/solution.py
@@ -141,6 +141,21 @@
     return jax.ShapeDtypeStruct(dims, dtype)
 
 
+def rows_call(arrays):
+    count = arrays[0].shape[1]
+    spots = [(n, r) for n, x in enumerate(arrays) for r in range(x.shape[0])]
+
+    def kernel(wait, *refs):
+        wait(*range(len(arrays)))
+        for (n, r), out_ref in zip(spots, refs[len(arrays) :]):
+            for k in range(count // LANES):
+                out_ref[k : k + 1] = refs[n][r : r + 1, k * LANES : (k + 1) * LANES]
+
+    outs = [shape((count // LANES, LANES))] * len(spots)
+    rows = call(kernel, "rows", outs, arrays, far=tuple(range(len(arrays))))
+    return [x.reshape(count) for x in rows]
+
+
 def expand_call(starts, keys, rows, devices, capacity, codes):
     count = keys.shape[1]
     wide = -(-capacity // LANES) * LANES + LANES
@@ -345,6 +360,12 @@
     return out
 
 
+def y_phase(table_ref, k, n1):
+    lanes = slice(k % 4 * LANES, k % 4 * LANES + LANES)
+    cos, sin = 4 * LANES + k // 4, 4 * LANES + (n1 + k) // 4
+    return table_ref[cos : cos + 1, lanes], table_ref[sin : sin + 1, lanes]
+
+
 def visit_windows(bound_ref, i, visit):
     first = pl.multiple_of(bound_ref[0, i] // LANES * LANES, LANES)
     visit(first, FIRST)
@@ -356,7 +377,7 @@
     lax.fori_loop(0, (bound_ref[1, i] - first - FIRST) // WINDOW + 1, step, 0)
 
 
-def project_call(field, bounds, rc, payload, table, tw_cos, tw_sin, x_local, grid_y):
+def project_call(field, bounds, rc, payload, table, x_local, grid_y):
     slots = rc.shape[1]
     chunks = bounds.shape[1]
     chunk = slots // chunks
@@ -365,8 +386,9 @@
     rows = k1l * x_local
     width = HALVES * 2 * LANES
     half = 4 * x_local
-
-    def kernel(wait, bound_ref, rc_ref, pay_ref, table_ref, cos_ref, sin_ref, out_ref, v_ref, acc_ref, x_ref):
+    height = 4 * LANES
+
+    def kernel(wait, bound_ref, rc_ref, pay_ref, table_ref, out_ref, v_ref, acc_ref, x_ref):
         @pl.loop(0, half // 32)
         def _(i):
             acc_ref[pl.ds(pl.multiple_of(i * 64, 64), 64)] = jnp.zeros((64, acc_ref.shape[1]), F32)
@@ -377,11 +399,11 @@
         def _(i):
             @pl.when(bound_ref[1, i] >= 0)
             def _():
-                @pl.loop(0, chunk // 256)
+                @pl.loop(0, chunk // 512)
                 def _(j):
-                    at = pl.ds(pl.multiple_of(i * chunk + j * 256, 256), 256)
-                    to = pl.ds(pl.multiple_of(j * 256, 256), 256)
-                    ids = lax.broadcasted_iota(jnp.int32, (x_local, 256), 0)
+                    at = pl.ds(pl.multiple_of(i * chunk + j * 512, 512), 512)
+                    to = pl.ds(pl.multiple_of(j * 512, 512), 512)
+                    ids = lax.broadcasted_iota(jnp.int32, (x_local, 512), 0)
                     m0 = ids == rc_ref[0:1, at]
                     m1 = ids == rc_ref[0:1, at] + 1
                     for c in range(2):
@@ -401,7 +423,7 @@
 
                 visit_windows(bound_ref, i, visit)
 
-        wait(3, 4, 5)
+        wait(3)
 
         @pl.loop(0, x_local // 8)
         def _(i):
@@ -416,31 +438,26 @@
                 parts.append([g[:, y * LANES : (y + 1) * LANES] for y in range(n1)])
             re, im = fft_list(parts[0], parts[1], -1.0)
             for k in range(n1):
-                cos, sin = cos_ref[k : k + 1, :], sin_ref[k : k + 1, :]
+                cos, sin = y_phase(table_ref, k, n1)
                 to = pl.ds(pl.multiple_of((k % k1l) * x_local + i * 8, 8), 8)
                 left = (k // k1l) * 2 * LANES
                 x_ref[to, left : left + LANES] = re[k] * cos + im[k] * sin
                 x_ref[to, left + LANES : left + 2 * LANES] = im[k] * cos - re[k] * sin
 
-        part = min(rows, 256)
-
-        @pl.loop(0, rows // part)
-        def _(j):
-            at = pl.ds(pl.multiple_of(j * part, part), part)
-            out_ref[:, at] = dot3(split(table_ref[...]), split(x_ref[at]), NT)
+        out_ref[...] = dot3(split(table_ref[:height]), split(x_ref[...]), NT)
 
     (out,) = call(
         kernel,
         "project",
-        [shape((table.shape[0], rows))],
-        [bounds, rc, payload, table, tw_cos, tw_sin],
+        [shape((height, rows))],
+        [bounds, rc, payload, table],
         scratch=[
             pltpu.VMEM((2 * half, chunk), BF16),
             pltpu.VMEM((2 * half, grid_y + FIRST), F32),
             pltpu.VMEM((rows, width), F32),
         ],
         smem_in=(0,),
-        far=(1, 2, 3, 4, 5),
+        far=(1, 2, 3),
         flops=4 * half * slots * grid_y,
     )
     return out
@@ -507,7 +524,7 @@
     return out
 
 
-def sample_call(data, bounds, rc, payload, table, tw_cos, tw_sin, x_local, grid_y, after):
+def sample_call(data, bounds, rc, payload, table, x_local, grid_y, after):
     slots = rc.shape[1]
     n1 = grid_y // LANES
     k1l = n1 // HALVES
@@ -516,23 +533,22 @@
     chunks = bounds.shape[1]
     chunk = slots // chunks
     half = 4 * x_local
-
-    def kernel(wait, in_ref, bound_ref, rc_ref, pay_ref, table_ref, cos_ref, sin_ref, out_ref, u_ref, g_ref, p_ref, t_ref):
+    height = 4 * LANES
+
+    def kernel(wait, in_ref, bound_ref, rc_ref, pay_ref, table_ref, out_ref, u_ref, g_ref, p_ref, t_ref):
         part = min(rows, 256)
         wait(4)
 
         @pl.loop(0, rows // part)
         def _(j):
             at = pl.ds(pl.multiple_of(j * part, part), part)
-            u_ref[at] = dot3(split(jnp.transpose(in_ref[:, at])), split(table_ref[...]), NN)
-
-        wait(5, 6)
+            u_ref[at] = dot3(split(jnp.transpose(in_ref[:, at])), split(table_ref[:height]), NN)
 
         @pl.loop(0, x_local // 8)
         def _(i):
             re, im = [], []
             for k in range(n1):
-                cos, sin = cos_ref[k : k + 1, :], sin_ref[k : k + 1, :]
+                cos, sin = y_phase(table_ref, k, n1)
                 at = pl.ds(pl.multiple_of((k % k1l) * x_local + i * 8, 8), 8)
                 left = (k // k1l) * 2 * LANES
                 a = u_ref[at, left : left + LANES]
@@ -597,7 +613,7 @@
         kernel,
         "sample",
         [shape((2, slots))],
-        [data, bounds, rc, payload, table, tw_cos, tw_sin],
+        [data, bounds, rc, payload, table],
         scratch=[
             pltpu.VMEM((rows, width), F32),
             pltpu.VMEM((2 * x_local, grid_y), F32),
@@ -605,7 +621,7 @@
             pltpu.VMEM((2 * half, chunk), F32),
         ],
         smem_in=(1,),
-        far=(2, 3, 4, 5, 6),
+        far=(2, 3, 4),
         flops=4 * half * slots * grid_y,
         after=after,
     )
@@ -658,7 +674,7 @@
     target = owner[:, 0]
     row, col = cell // grid_y % (x_local - 1), cell % grid_y
     key = target * codes + col * x_local + row
-    columns = [*currents, *probes, *proj_weights, *interp_weights]
+    columns = rows_call([currents, probes, proj_weights, interp_weights])
     order = lax.iota(jnp.int32, elem_count)
     key, *columns, order = lax.sort((key, *columns, order), num_keys=1, is_stable=False)
     bounds_of = jnp.arange(devices + 1, dtype=jnp.int32)
@@ -669,8 +685,8 @@
     arrived = lax.all_to_all(outgoing, AXES, split_axis=0, concat_axis=0, tiled=True)
     payload, rc, bounds, held = gather_groups(arrived, x_local, CHUNK)
 
-    table = jnp.asarray(y_table(devices, per), F32)
-    ty_cos, ty_sin = (jnp.asarray(t, F32) for t in phases(n1, LANES, grid_y))
+    twiddles = np.concatenate(phases(n1, LANES, grid_y)).reshape(-1, 4 * LANES)
+    table = jnp.asarray(np.concatenate([y_table(devices, per), twiddles]), F32)
     tx_cos, tx_sin = (
         jnp.asarray(np.tile(t, (1, k1l)), F32) for t in phases(devices, x_local, grid_x)
     )
@@ -694,12 +710,12 @@
 
     def sample(products, *after):
         return sample_call(
-            products, bounds, rc, payload, table, ty_cos, ty_sin, x_local, grid_y, after
+            products, bounds, rc, payload, table, x_local, grid_y, after
         )
 
     spectra = []
     for field in range(3):
-        grids = project_call(field, bounds, rc, payload, table, ty_cos, ty_sin, x_local, grid_y)
+        grids = project_call(field, bounds, rc, payload, table, x_local, grid_y)
         spectra.extend(exchange(grids))
     products = exchange(spectral(spectra[0]), spectral(spectra[1]))
     products += exchange(spectral(spectra[2]))

time: 279 us -> 275 us (0.986)
  Pallas kernels: 88 us -> 101 us
  starting transfers between devices: 31.6 us -> 26 us
  local copies, waits for them, and re-layouts: 27.7 us -> 22.1 us
  waiting for transfers between devices: 81 us -> 75.9 us
    pallas_call x13 -> x14, Pallas kernels: 88 us -> 101 us  [call(): pl.pallas_call(body, out_shape=list(out_shape), in_specs=[pl.BlockSpec(me...]
    all_to_all x5, waiting for transfers between devices: 73.8 us -> 68.6 us  [exchange(): lax.all_to_all(jnp.concatenate(shaped, axis=1), AXES, split_axis=0, conca...]
    another operation x4 -> x0, local copies, waits for them, and re-layouts: 4.12 us -> none  [on_device(): columns = [*currents, *probes, *proj_weights, *interp_weights]]
    all_to_all x1, starting transfers between devices: 13.3 us -> 9.93 us  [on_device(): lax.all_to_all(returning, AXES, split_axis=0, concat_axis=0, tiled=True)]
    unnamed x58 -> x52, local copies, waits for them, and re-layouts: 13.1 us -> 11.5 us
  transfers between devices with their start and end apart: 6 -> 6, of which waited for: 6 -> 6; matrix products, arithmetic and copies ran while one was open for 8% -> 8% of each run, Pallas kernels for 20% -> 24%
where the time goes in v1:
time: 275 us; the launch traced here: 274 us
  Pallas kernels  101 us (37%)
  waiting for transfers between devices  75.9 us (28%)
  starting transfers between devices  26 us (9%)
  blocking collectives  23.5 us (9%)
  local copies, waits for them, and re-layouts  22.1 us (8%)
  other arithmetic  17.2 us (6%)
  matrix products  6.86 us (2%)
    pallas_call x14, Pallas kernels, call(): pl.pallas_call(body, out_shape=list(out_shape), in_specs=[pl.BlockSpec(me...  101 us
    all_to_all x5, waiting for transfers between devices, exchange(): lax.all_to_all(jnp.concatenate(shaped, axis=1), AXES, split_axis=0, conca...  68.6 us
    all_to_all x1, blocking collectives, on_device(): lax.all_to_all(outgoing, AXES, split_axis=0, concat_axis=0, tiled=True)  23.5 us
    all_to_all x5, starting transfers between devices, exchange(): lax.all_to_all(jnp.concatenate(shaped, axis=1), AXES, split_axis=0, conca...  16.1 us
    unnamed x52, local copies, waits for them, and re-layouts  11.5 us
    all_to_all x1, starting transfers between devices, on_device(): lax.all_to_all(returning, AXES, split_axis=0, concat_axis=0, tiled=True)  9.93 us
    all_to_all x1, waiting for transfers between devices, on_device(): lax.all_to_all(returning, AXES, split_axis=0, concat_axis=0, tiled=True)  7.23 us
    mul x2, local copies, waits for them, and re-layouts, on_device(): jnp.transpose(kernel_view, (4, 1, 0, 2, 3)) * (1.0 / (grid_x * grid_y))  6.37 us
  transfers between devices with their start and end apart: 6, of which 6 were waited for; matrix products, arithmetic and copies ran while one was open for 8% of the time, Pallas kernels for 24%

profile of v1, /device:TPU:0, one launch (start us, length us, event | category | flops | bytes accessed | tf_op | source)
XLA Modules:
  0.0 273.7 jit_solution(10798760277264369191)
XLA Ops:
  0.6 0.9 convert_reduce_fusion.refs_0_
  1.5 0.8 fusion.18
  2.3 0.8 copy-done.3
  3.1 0.8 copy-done.5
  4.0 0.8 copy-done.7
  4.8 0.8 copy-done.8
  5.7 0.5 rows.1
  6.2 5.4 %sort.144 = (s32[4096]{0:T(1024)S(1)}, f32[4096]{0:T(1024)S(1)}, f32[4096]{0:T(1024)S(1)}, f32[4096]{0:T(1024)S(1)}, f32[4096]{0:T(1024)S(1)}, /*index=5*/f32[40...) sort(s32[4096]{0:T(1024)S(1)} %fusion.18, ...), dimensions={0}, to_apply=%region_0.1 | sort | flops 49152 | bytes 524288 | tf_op jit(solution)/shard_map/sort | solution.py:679
  11.6 1.5 expand.1
  13.1 23.5 %all_to_all.35.refs_0_ = f32[32,16,256]{2,1,0:T(8,128)S(1)} all-to-all(f32[32,16,256]{2,1,0:T(8,128)S(1)} %expand.1), channel_id=1, replica_groups=mesh['row'=4,'col'=8] {'row','col'}, dimensions={0} | all-to-all | bytes 1048576 | tf_op jit(solution)/shard_map/all_to_all | solution.py:685
  36.6 4.3 %groups.1 = (f32[16,8192]{1,0:T(8,128)S(1)}, s32[2,8192]{1,0:T(2,128)S(1)}, s32[2,8]{1,0:T(2,128)S(1)}, f32[40,128]{1,0:T(8,128)S(1)}) custom-call(f32[32,16,256]{2,1,0:T(8,128)S(1)} %all_to_all.35.refs_0_), custom_call_target="tpu_custom_call" | custom-call | bytes 1134656 | tf_op jit(solution)/shard_map/groups/pallas_call | solution.py:127
  40.9 13.4 %project.3 = f32[512,512]{1,0:T(8,128)} custom-call(s32[2,8]{1,0:T(2,128)S(1)} %get-tuple-element.72.refs_0_.refs_1_, s32[2,8192]{1,0:T(2,128)S(1)} %get-tuple-element.73.refs_1_.refs_2_, f32[16,8192]{1,0:T(8,128)S(1)} %get-tuple-element.74.refs_2_.refs_3_, f32[520,512]{1,0:T(8,128)S(1)} %copy-done.11), custom_call_target="tpu_custom_call" | custom-call | flops 17179869184 | bytes 2703424 | tf_op jit(solution)/shard_map/project/pallas_call | solution.py:127
  54.3 3.7 %all-to-all-start.1 = ((f32[32,16,512]{2,1,0:T(8,128)}), f32[32,16,512]{2,1,0:T(8,128)S(1)}, u32[]{:S(2)}, u32[]{:S(2)}) async-start(f32[32,16,512]{2,1,0:T(8,128)} %bitcast.30), calls=%async_computation.1 | async-start | bytes 2097152 | tf_op jit(solution)/shard_map/all_to_all | solution.py:702
  58.0 0.0 copy-start.12
  58.0 1.2 copy-done.12
  59.2 13.4 %project.4 = f32[512,512]{1,0:T(8,128)} custom-call(s32[2,8]{1,0:T(2,128)S(1)} %get-tuple-element.72.refs_0_.refs_1_, s32[2,8192]{1,0:T(2,128)S(1)} %get-tuple-element.73.refs_1_.refs_2_, f32[16,8192]{1,0:T(8,128)S(1)} %get-tuple-element.74.refs_2_.refs_3_, f32[520,512]{1,0:T(8,128)S(1)} %copy-done.12), custom_call_target="tpu_custom_call" | custom-call | flops 17179869184 | bytes 2703424 | tf_op jit(solution)/shard_map/project/pallas_call | solution.py:127
  72.6 13.0 %all-to-all-done.1 = f32[32,16,512]{2,1,0:T(8,128)S(1)} async-done(((f32[32,16,512]{2,1,0:T(8,128)}), f32[32,16,512]{2,1,0:T(8,128)S(1)}, u32[]{:S(2)}, u32[]{:S(2)}) %all-to-all-start.1) | async-done | bytes 1048608 | tf_op jit(solution)/shard_map/all_to_all | solution.py:702
  85.6 2.8 %all-to-all-start.2 = ((f32[32,16,512]{2,1,0:T(8,128)}), f32[32,16,512]{2,1,0:T(8,128)S(1)}, u32[]{:S(2)}, u32[]{:S(2)}) async-start(f32[32,16,512]{2,1,0:T(8,128)} %bitcast.34), calls=%async_computation.2 | async-start | bytes 2097152 | tf_op jit(solution)/shard_map/all_to_all | solution.py:702
  88.4 0.0 copy-start.13
  88.4 1.2 copy-done.13
  89.7 12.4 %project.5 = f32[512,512]{1,0:T(8,128)S(1)} custom-call(s32[2,8]{1,0:T(2,128)S(1)} %get-tuple-element.72.refs_0_.refs_1_, s32[2,8192]{1,0:T(2,128)S(1)} %get-tuple-element.73.refs_1_.refs_2_, f32[16,8192]{1,0:T(8,128)S(1)} %get-tuple-element.74.refs_2_.refs_3_, f32[520,512]{1,0:T(8,128)S(1)} %copy-done.13), custom_call_target="tpu_custom_call" | custom-call | flops 17179869184 | bytes 2703424 | tf_op jit(solution)/shard_map/project/pallas_call | solution.py:127
  102.0 1.0 copy-done
  103.0 12.8 %all-to-all-done.2 = f32[32,16,512]{2,1,0:T(8,128)S(1)} async-done(((f32[32,16,512]{2,1,0:T(8,128)}), f32[32,16,512]{2,1,0:T(8,128)S(1)}, u32[]{:S(2)}, u32[]{:S(2)}) %all-to-all-start.2) | async-done | bytes 1048608 | tf_op jit(solution)/shard_map/all_to_all | solution.py:702
  115.8 2.6 all-to-all-start.4
  118.5 1.9 broadcast_multiply_fusion
  120.3 3.0 %mul.30 = f32[4,2,8,64,32]{4,3,2,1,0:T(8,128)} reshape(f32[1,64,2048]{2,1,0:T(8,128)} %broadcast_multiply_fusion) | data formatting | bytes 1048576 | tf_op jit(solution)/shard_map/mul | solution.py:696
  123.3 3.4 %copy.26 = f32[32,2,4,8,64]{4,3,2,1,0:T(8,128)} copy(f32[32,2,4,8,64]{0,4,3,1,2:T(8,128)} %bitcast.145) | data formatting | bytes 1048576 | tf_op jit(solution)/shard_map/mul | solution.py:696
  126.7 2.3 reshape.118.refs_1_
  129.0 1.0 copy-done.1
  130.0 0.9 copy-done.17
  131.0 0.9 copy-done.19
  131.9 0.8 copy-done.21
  132.7 0.8 copy-done.23
  133.5 4.5 %spectral.3 = f32[512,512]{1,0:T(8,128)S(1)} custom-call(f32[512,512]{1,0:T(8,128)S(1)} %bitcast.107, f32[256,512]{1,0:T(8,128)S(1)} %copy-done.1, bf16[256,256]{1,0:T(8,128)(2,1)S(1)} %copy-done.15, bf16[256,256]{1,0:T(8,128)(2,1)S(1)} %copy-done.16, bf16[256,256]{1,0:T(8,128)(2,1)S(1)} %copy-done.17, bf16[256,256]{1,0:T(8,128)(2,1)S(1)} %copy-done.19, ...), custom_call_target="tpu_custom_call" | custom-call | flops 1073741824 | bytes 3276800 | tf_op jit(solution)/shard_map/spectral/pallas_call | solution.py:127
  138.0 4.5 %spectral.4 = f32[512,512]{1,0:T(8,128)S(1)} custom-call(f32[512,512]{1,0:T(8,128)S(1)} %bitcast.108, f32[256,512]{1,0:T(8,128)S(1)} %copy-done.1, bf16[256,256]{1,0:T(8,128)(2,1)S(1)} %copy-done.15, bf16[256,256]{1,0:T(8,128)(2,1)S(1)} %copy-done.16, bf16[256,256]{1,0:T(8,128)(2,1)S(1)} %copy-done.17, bf16[256,256]{1,0:T(8,128)(2,1)S(1)} %copy-done.19, ...), custom_call_target="tpu_custom_call" | custom-call | flops 1073741824 | bytes 3276800 | tf_op jit(solution)/shard_map/spectral/pallas_call | solution.py:127
  142.5 1.6 pad_maximum_fusion
  144.2 1.9 all-to-all-done.4
  146.1 4.1 %all-to-all-start.3 = ((f32[32,32,512]{2,1,0:T(8,128)}), f32[32,32,512]{2,1,0:T(8,128)}, u32[]{:S(2)}, u32[]{:S(2)}) async-start(f32[32,32,512]{2,1,0:T(8,128)} %pad_maximum_fusion), calls=%async_computation.3 | async-start | bytes 4194304 | tf_op jit(solution)/shard_map/all_to_all | solution.py:702
  150.2 0.0 copy-start.18
  150.2 0.0 copy-start.20
  150.2 0.0 copy-start.22
  150.3 0.0 copy-start.24
  150.3 2.9 %convolution_bitcast_fusion = f32[6,32,4,128]{3,0,2,1:T(8,128)S(1)} fusion(bf16[32,4,128,128]{3,2,1,0:T(8,128)(2,1)} %param.23, bf16[3,32,128]{2,0,1:T(4,128)(2,1)S(1)} %get-tuple-element.93, bf16[3,32,128]{2,0,1:T(4,128)(2,1)S(1)} %get-tuple-element.92), kind=kOutput, calls=%fused_computation.1 | convolution fusion | flops 25264128 | bytes 4636672 | tf_op jit(solution)/shard_map/cbi,bnij->cbnj/dot_general | solution.py:647
  153.2 0.1 slice_add_fusion
  153.3 0.3 convolution_bitcast_fusion.3
  153.6 0.3 reduce-precision_convert_fusion
  153.9 5.5 %spectral.5 = f32[512,512]{1,0:T(8,128)} custom-call(f32[512,512]{1,0:T(8,128)S(1)} %bitcast.106, f32[256,512]{1,0:T(8,128)S(1)} %copy-done.2, bf16[256,256]{1,0:T(8,128)(2,1)S(1)} %copy-done.15, bf16[256,256]{1,0:T(8,128)(2,1)S(1)} %copy-done.16, bf16[256,256]{1,0:T(8,128)(2,1)S(1)} %copy-done.18, bf16[256,256]{1,0:T(8,128)(2,1)S(1)} %copy-done.20, ...), custom_call_target="tpu_custom_call" | custom-call | flops 1073741824 | bytes 3276800 | tf_op jit(solution)/shard_map/spectral/pallas_call | solution.py:127
  159.4 40.8 %all-to-all-done.3 = f32[32,32,512]{2,1,0:T(8,128)} async-done(((f32[32,32,512]{2,1,0:T(8,128)}), f32[32,32,512]{2,1,0:T(8,128)}, u32[]{:S(2)}, u32[]{:S(2)}) %all-to-all-start.3) | async-done | bytes 2097184 | tf_op jit(solution)/shard_map/all_to_all | solution.py:702
  200.2 2.9 %all-to-all-start.5 = ((f32[32,16,512]{2,1,0:T(8,128)}), f32[32,16,512]{2,1,0:T(8,128)S(1)}, u32[]{:S(2)}, u32[]{:S(2)}) async-start(f32[32,16,512]{2,1,0:T(8,128)} %bitcast.41), calls=%async_computation.5 | async-start | bytes 2097152 | tf_op jit(solution)/shard_map/all_to_all | solution.py:702
  203.1 1.9 fusion.23
  205.0 0.1 copy-done.14
  205.1 12.6 %sample.4.refs_6_ = f32[2,8192]{1,0:T(2,128)S(1)} custom-call(f32[512,512]{1,0:T(8,128)S(1)} %bitcast.113, s32[2,8]{1,0:T(2,128)S(1)} %get-tuple-element.72.refs_0_.refs_1_, s32[2,8192]{1,0:T(2,128)S(1)} %get-tuple-element.73.refs_1_.refs_2_, f32[16,8192]{1,0:T(8,128)S(1)} %copy-done.10, f32[520,512]{1,0:T(8,128)S(1)} %copy-done.14), custom_call_target="tpu_custom_call" | custom-call | flops 17179869184 | bytes 2768960 | tf_op jit(solution)/shard_map/sample/pallas_call | solution.py:127
  217.7 12.6 %sample.3.refs_5_ = f32[2,8192]{1,0:T(2,128)S(1)} custom-call(f32[512,512]{1,0:T(8,128)S(1)} %bitcast.111, s32[2,8]{1,0:T(2,128)S(1)} %get-tuple-element.72.refs_0_.refs_1_, s32[2,8192]{1,0:T(2,128)S(1)} %get-tuple-element.73.refs_1_.refs_2_, f32[16,8192]{1,0:T(8,128)S(1)} %copy-done.10, f32[520,512]{1,0:T(8,128)S(1)} %copy-done.14), custom_call_target="tpu_custom_call" | custom-call | flops 17179869184 | bytes 2768960 | tf_op jit(solution)/shard_map/sample/pallas_call | solution.py:127
  230.3 0.1 all-to-all-done.5
  230.5 12.6 %sample.5 = f32[2,8192]{1,0:T(2,128)S(1)} custom-call(f32[512,512]{1,0:T(8,128)S(1)} %bitcast.110, s32[2,8]{1,0:T(2,128)S(1)} %get-tuple-element.72.refs_0_.refs_1_, s32[2,8192]{1,0:T(2,128)S(1)} %get-tuple-element.73.refs_1_.refs_2_, f32[16,8192]{1,0:T(8,128)S(1)} %copy-done.10, f32[520,512]{1,0:T(8,128)S(1)} %copy-done.14, f32[2,8192]{1,0:T(2,128)S(1)} %sample.3.refs_5_, ...), custom_call_target="tpu_custom_call" | custom-call | flops 17179869184 | bytes 2768960 | tf_op jit(solution)/shard_map/sample/pallas_call | solution.py:127
  243.0 0.1 pad_maximum_fusion.1.refs_0_
  243.1 1.8 ungroup.1
  244.9 9.9 %all-to-all-start.6 = ((f32[32,6,256]{2,1,0:T(8,128)}), f32[32,6,256]{2,1,0:T(8,128)S(1)}, u32[]{:S(2)}, u32[]{:S(2)}) async-start(f32[32,6,256]{2,1,0:T(8,128)} %ungroup.1), calls=%async_computation.6 | async-start | bytes 524288 | tf_op jit(solution)/shard_map/all_to_all | solution.py:727
  254.9 3.4 %convolution_bitcast_fusion.2 = f32[6,32,128]{2,0,1:T(8,128)S(1)} fusion(bf16[32,4,128,128]{3,2,1,0:T(8,128)(2,1)} %param.23, bf16[6,32,4,128]{3,1,0,2:T(8,128)(2,1)S(1)} %pad_maximum_fusion.2), kind=kOutput, calls=%fused_computation.3 | convolution fusion | flops 25165824 | bytes 4489216 | tf_op jit(solution)/shard_map/cbnj,bnij->cbi/dot_general | solution.py:643
  258.2 7.2 %all-to-all-done.6.refs_1_ = f32[32,6,256]{2,1,0:T(8,128)S(1)} async-done(((f32[32,6,256]{2,1,0:T(8,128)}), f32[32,6,256]{2,1,0:T(8,128)S(1)}, u32[]{:S(2)}, u32[]{:S(2)}) %all-to-all-start.6) | async-done | bytes 196640 | tf_op jit(solution)/shard_map/all_to_all | solution.py:727
  265.5 1.7 compact.1
  267.2 0.1 fusion.24
  267.3 5.6 %sort.145 = (s32[4096]{0:T(1024)}, f32[4096]{0:T(1024)S(1)}, f32[4096]{0:T(1024)S(1)}, f32[4096]{0:T(1024)S(1)}, f32[4096]{0:T(1024)S(1)}, /*index=5*/f32[4096]{0:T(1024)S(1)}, f32[4096]{0:T(1024)S(1)}) sort(s32[4096]{0:T(1024)S(1)} %get-tuple-element.56, f32[4096]{0:T(1024)S(1)} %bitcast.151, f32[4096]{0:T(1024)S(1)} %bitcast.150, f32[4096]{0:T(1024)S(1)} %bitcast.149, ...), dimensions={0}, to_apply=%region_2.3 | sort | flops 49152 | bytes 229376 | tf_op jit(solution)/shard_map/sort | solution.py:729
  272.9 0.8 bitcast_add_fusion
  (36 shorter events, 0.1 us)
Async XLA Ops:
  2.3 0.8 copy-start.3
  3.1 0.8 copy-start.5
  4.0 0.8 copy-start.7
  4.8 0.8 copy-start.8
  5.7 35.2 %copy-start.11 = (f32[520,512]{1,0:T(8,128)S(1)}, f32[520,512]{1,0:T(8,128)}, u32[]{:S(2)}) copy-start(f32[520,512]{1,0:T(8,128)} %constant.57.clone.refs_3_.refs_4_) | copy-start | bytes 3194884
  40.9 47.5 %copy-start.9 = (f32[16,8192]{1,0:T(8,128)}, f32[16,8192]{1,0:T(8,128)S(1)}, u32[]{:S(2)}) copy-start(f32[16,8192]{1,0:T(8,128)S(1)} %get-tuple-element.74.refs_2_.refs_3_) | copy-start | bytes 1572868
  54.3 31.3 %all-to-all-start.1 = ((f32[32,16,512]{2,1,0:T(8,128)}), f32[32,16,512]{2,1,0:T(8,128)S(1)}, u32[]{:S(2)}, u32[]{:S(2)}) async-start(f32[32,16,512]{2,1,0:T(8,128)} %bitcast.30), calls=%async_computation.1 | async-start | bytes 2097152 | tf_op jit(solution)/shard_map/all_to_all | solution.py:702
  58.0 1.2 copy-start.12
  85.6 30.2 %all-to-all-start.2 = ((f32[32,16,512]{2,1,0:T(8,128)}), f32[32,16,512]{2,1,0:T(8,128)S(1)}, u32[]{:S(2)}, u32[]{:S(2)}) async-start(f32[32,16,512]{2,1,0:T(8,128)} %bitcast.34), calls=%async_computation.2 | async-start | bytes 2097152 | tf_op jit(solution)/shard_map/all_to_all | solution.py:702
  88.4 1.2 copy-start.13
  102.0 1.0 copy-start
  115.8 30.2 %all-to-all-start.4 = ((f32[32,16,512]{2,1,0:T(8,128)}), f32[32,16,512]{2,1,0:T(8,128)S(1)}, u32[]{:S(2)}, u32[]{:S(2)}) async-start(f32[32,16,512]{2,1,0:T(8,128)} %bitcast.109), calls=%async_computation.4 | async-start | bytes 2097152 | tf_op jit(solution)/shard_map/all_to_all | solution.py:702
  123.3 5.7 %copy-start.15 = (bf16[256,256]{1,0:T(8,128)(2,1)S(1)}, bf16[256,256]{1,0:T(8,128)(2,1)}, u32[]{:S(2)}) copy-start(bf16[256,256]{1,0:T(8,128)(2,1)} %constant.60.clone.refs_2_) | copy-start | bytes 393220
  123.3 5.7 %copy-start.16 = (bf16[256,256]{1,0:T(8,128)(2,1)S(1)}, bf16[256,256]{1,0:T(8,128)(2,1)}, u32[]{:S(2)}) copy-start(bf16[256,256]{1,0:T(8,128)(2,1)} %constant.61.clone.refs_3_) | copy-start | bytes 393220
  129.0 1.0 copy-start.1
  130.0 0.9 copy-start.17
  131.0 0.9 copy-start.19
  131.9 0.8 copy-start.21
  132.7 0.8 copy-start.23
  144.2 6.0 %copy-start.4 = (f32[3,4096]{1,0:T(4,128)S(1)}, f32[3,4096]{1,0:T(4,128)}, u32[]{:S(2)}) copy-start(f32[3,4096]{1,0:T(4,128)} %refs_1_.1) | copy-start | bytes 147460
  146.1 54.2 %all-to-all-start.3 = ((f32[32,32,512]{2,1,0:T(8,128)}), f32[32,32,512]{2,1,0:T(8,128)}, u32[]{:S(2)}, u32[]{:S(2)}) async-start(f32[32,32,512]{2,1,0:T(8,128)} %pad_maximum_fusion), calls=%async_computation.3 | async-start | bytes 4194304 | tf_op jit(solution)/shard_map/all_to_all | solution.py:702
  150.2 3.1 %copy-start.25 = (s32[32,4]{0,1:T(4,128)S(1)}, s32[32,4]{0,1:T(4,128)}, u32[]{:S(2)}) copy-start(s32[32,4]{0,1:T(4,128)} %param.22) | copy-start | bytes 1540
  150.2 3.4 %copy-start.6 = (f32[3,4096]{1,0:T(4,128)S(1)}, f32[3,4096]{1,0:T(4,128)}, u32[]{:S(2)}) copy-start(f32[3,4096]{1,0:T(4,128)} %refs_0_.1) | copy-start | bytes 147460
  150.2 3.7 %copy-start.2 = (f32[256,512]{1,0:T(8,128)S(1)}, f32[256,512]{1,0:T(8,128)}, u32[]{:S(2)}) copy-start(f32[256,512]{1,0:T(8,128)} %reshape.118.refs_1_) | copy-start | bytes 1572868
  150.2 3.7 %copy-start.18 = (bf16[256,256]{1,0:T(8,128)(2,1)S(1)}, bf16[256,256]{1,0:T(8,128)(2,1)}, u32[]{:S(2)}) copy-start(bf16[256,256]{1,0:T(8,128)(2,1)} %constant.62.clone.refs_4_) | copy-start | bytes 393220
  150.2 3.7 %copy-start.20 = (bf16[256,256]{1,0:T(8,128)(2,1)S(1)}, bf16[256,256]{1,0:T(8,128)(2,1)}, u32[]{:S(2)}) copy-start(bf16[256,256]{1,0:T(8,128)(2,1)} %constant.63.clone.refs_5_) | copy-start | bytes 393220
  150.2 3.6 %copy-start.22 = (f32[32,512]{1,0:T(8,128)S(1)}, f32[32,512]{1,0:T(8,128)}, u32[]{:S(2)}) copy-start(f32[32,512]{1,0:T(8,128)} %constant.58.clone.refs_6_) | copy-start | bytes 196612
  150.3 3.6 %copy-start.24 = (f32[32,512]{1,0:T(8,128)S(1)}, f32[32,512]{1,0:T(8,128)}, u32[]{:S(2)}) copy-start(f32[32,512]{1,0:T(8,128)} %constant.59.clone.refs_7_) | copy-start | bytes 196612
  200.2 30.2 %all-to-all-start.5 = ((f32[32,16,512]{2,1,0:T(8,128)}), f32[32,16,512]{2,1,0:T(8,128)S(1)}, u32[]{:S(2)}, u32[]{:S(2)}) async-start(f32[32,16,512]{2,1,0:T(8,128)} %bitcast.41), calls=%async_computation.5 | async-start | bytes 2097152 | tf_op jit(solution)/shard_map/all_to_all | solution.py:702
  203.1 1.9 copy-start.10
  203.1 2.0 copy-start.14
  244.9 20.6 %all-to-all-start.6 = ((f32[32,6,256]{2,1,0:T(8,128)}), f32[32,6,256]{2,1,0:T(8,128)S(1)}, u32[]{:S(2)}, u32[]{:S(2)}) async-start(f32[32,6,256]{2,1,0:T(8,128)} %ungroup.1), calls=%async_computation.6 | async-start | bytes 524288 | tf_op jit(solution)/shard_map/all_to_all | solution.py:727
